TPU v7x, 32 devices: a whole 2x2x4 slice. The times are simulated.
32 devices in a mesh: tile: 16 (over z, x, core), case: 2 (over y).
Axes of the slice: x: 2, y: 2, z: 4, core: 2. Of those that a mesh axis runs over, the one named last changes fastest.
Arguments:
- load: float32 [4, 3, 24576], P('case', None, 'tile')
- target: float32 [4, 3, 24576], P('case', None, 'tile'), may hold values from -6 to 6
- lame_lambda: float32 [24576], P('tile'), may hold values from 0.5 to 2
- lame_mu: float32 [24576], P('tile'), may hold values from 0.5 to 2
- volume: float32 [24576], P('tile'), may hold values from 0.5 to 2
- smooth: float32 [192, 4, 3, 128, 128], P('tile'), may hold values from -0.25 to 0.25
- columns: int32 [192, 4], P('tile'), may hold values from 0 to 27, as said below
- send_list: int32 [16, 2, 8], P('tile'), may hold values from 0 to 11, as said below
- counts: int32 [16], P('tile'), may hold values from 192 to 1536, as said below
Outputs:
- displacement: float32 [4, 3, 24576], P('case', None, 'tile')
- grad_lambda: float32 [24576], P('tile')
- grad_mu: float32 [24576], P('tile')
Inputs may be any that keep to these rules, and one draw needn't show every extreme that they name: `columns`: slot 0 of every block names the block itself (its index within the tile); in every tile, slot 3 of block 0 names pool block 12 and slot 3 of block 11 names pool block 27; the other slots name any block of the pool. Entries send_list[t, 1, 0] and send_list[t, 0, 7] are never 0. `counts`: some tile is full.
All inputs are finite; a program needn't handle non-finite values.
Results may differ from a plain program's by a relative error of at most 0.0001.
Values sent between devices are 32-bit elements; how exact they have to be, the bound alone decides.
No kernel may reach another device: no remote copies, remote signals or barrier semaphores. Data moves between devices by JAX's collectives and lax.ppermute only.
A program may use at most 64 MiB of HBM per device.

v0:
```python
import jax
import jax.numpy as jnp
from jax import lax
from jax.sharding import PartitionSpec as P

ITERS = 6
HIGH = lax.Precision.HIGHEST
KAPPA = 0.5


def extended(shard, sides, width):
    for axis, dim in sides:
        size, length = (lax.axis_size(axis), shard.shape[dim])
        up = [(i, (i + 1) % size) for i in range(size - 1)]
        down = [(j, i) for i, j in up]
        last = lax.slice_in_dim(shard, length - width, length, axis=dim)
        leading = lax.slice_in_dim(shard, 0, width, axis=dim)
        before = lax.ppermute(last, axis, up)
        after = lax.ppermute(leading, axis, down)
        shard = jnp.concatenate([before, shard, after], axis=dim)
    return shard


def shards(load, target, lame_lambda, lame_mu, volume, smooth, columns, send_list, counts):
    cases = load.shape[0]
    nblk = smooth.shape[0]
    ghosts = send_list.shape[2]
    width = smooth.shape[3]
    pool_n = nblk + 2 * ghosts
    field_shape = (cases, 3, nblk, width)
    alive = (
        (jnp.arange(nblk * width, dtype=jnp.int32) < counts[0])
        .astype(jnp.float32)
        .reshape(nblk, width)
    )
    weight = volume.reshape(nblk, width) * alive
    lam_weight = weight * lame_lambda.reshape(nblk, width)
    shear_weight = weight * lame_mu.reshape(nblk, width)
    column_hot = (columns[:, :, None] == jnp.arange(pool_n, dtype=jnp.int32)[None, None, :]).astype(
        jnp.float32
    )
    block_range = jnp.arange(nblk, dtype=jnp.int32)
    identity = jnp.eye(3, dtype=jnp.float32)
    neighbors = extended(send_list, (("tile", 0),), 1)
    below_ids = neighbors[0, 1]
    above_ids = neighbors[2, 0]
    below_hot = (below_ids[:, None] == block_range[None, :]).astype(jnp.float32)
    above_hot = (above_ids[:, None] == block_range[None, :]).astype(jnp.float32)

    def collect(field):
        padded = extended(field, (("tile", 2),), nblk)
        from_left = jnp.take(padded[:, :, :nblk], below_ids, axis=2)
        from_right = jnp.take(padded[:, :, 2 * nblk :], above_ids, axis=2)
        return jnp.concatenate([field, from_left, from_right], axis=2)

    def send_back(lower_part, upper_part):
        to_lower = jnp.einsum("cegj,gb->cebj", lower_part, below_hot, precision=HIGH)
        to_upper = jnp.einsum("cegj,gb->cebj", upper_part, above_hot, precision=HIGH)
        padded = extended(jnp.concatenate([to_lower, to_upper], axis=2), (("tile", 2),), nblk)
        return padded[:, :, :nblk] + padded[:, :, 3 * nblk :]

    def strains(field):
        pooled = collect(field * alive)
        gathered = jnp.einsum("ceqj,bkq->cebkj", pooled, column_hot, precision=HIGH)
        return jnp.einsum("bkdij,cebkj->cedbi", smooth, gathered, precision=HIGH)

    def operate(field):
        grads = strains(field)
        trace_u = grads[:, 0, 0] + grads[:, 1, 1] + grads[:, 2, 2]
        strain = 0.5 * (grads + jnp.swapaxes(grads, 1, 2))
        stress = (
            2.0 * shear_weight * strain
            + (lam_weight * trace_u)[:, None, None] * identity[None, :, :, None, None]
        )
        contrib = jnp.einsum("bkdij,cedbi->cebkj", smooth, stress, precision=HIGH)
        pooled = jnp.einsum("cebkj,bkq->ceqj", contrib, column_hot, precision=HIGH)
        own = pooled[:, :, :nblk]
        returned = send_back(pooled[:, :, nblk : nblk + ghosts], pooled[:, :, nblk + ghosts :])
        return alive * (own + returned) + KAPPA * field

    def curvature(first, second):
        return lax.psum(jnp.sum(first * second, axis=(1, 2, 3)), "tile")

    def squares(residual):
        return lax.psum(jnp.sum(residual * residual, axis=(1, 2, 3)), "tile")

    def widen(scalars):
        return scalars[:, None, None, None]

    def run_solver(rhs):
        solution = jnp.zeros_like(rhs)
        residual = rhs
        direction = rhs
        norm_now = squares(residual)
        for sweep in range(ITERS):
            image = operate(direction)
            step_len = norm_now / curvature(direction, image)
            solution = solution + widen(step_len) * direction
            residual = residual - widen(step_len) * image
            norm_next = squares(residual)
            direction = residual + widen(norm_next / norm_now) * direction
            norm_now = norm_next
        return solution

    forward = run_solver(alive * load.reshape(field_shape))
    adjoint = run_solver(alive * (forward - target.reshape(field_shape)))
    grads = strains(jnp.concatenate([forward, adjoint], axis=0))
    grads_u = grads[:cases]
    grads_a = grads[cases:]
    trace_u = grads_u[:, 0, 0] + grads_u[:, 1, 1] + grads_u[:, 2, 2]
    trace_a = grads_a[:, 0, 0] + grads_a[:, 1, 1] + grads_a[:, 2, 2]
    strain_u = 0.5 * (grads_u + jnp.swapaxes(grads_u, 1, 2))
    strain_a = 0.5 * (grads_a + jnp.swapaxes(grads_a, 1, 2))
    local_lambda = (-weight * jnp.sum(trace_u * trace_a, axis=0)).reshape(-1)
    local_mu = (-2.0 * weight * jnp.sum(strain_u * strain_a, axis=(0, 1, 2))).reshape(-1)
    grad_lambda, grad_mu = lax.psum((local_lambda, local_mu), "case")
    return (forward.reshape(load.shape), grad_lambda, grad_mu)


def solution(mesh):
    return jax.shard_map(
        shards,
        mesh=mesh,
        in_specs=(
            P("case", None, "tile"),
            P("case", None, "tile"),
            P("tile"),
            P("tile"),
            P("tile"),
            P("tile", None, None, None, None),
            P("tile", None),
            P("tile", None, None),
            P("tile"),
        ),
        out_specs=(P("case", None, "tile"), P("tile"), P("tile")),
        check_vma=False,
    )
```

profile of v0, /device:TPU:0, one launch (start us, length us, event | category | flops | bytes accessed | tf_op | source)
XLA Modules:
  0.0 1096.6 jit_solution(6777021464076940048)
XLA Ops:
  5.8 5.1 collective-permute-start.1
  18.0 11.6 %fusion.48 = f32[12,2,3,3,128,1]{4,2,5,3,1,0:T(4,128)S(1)} fusion(f32[12,4,2,3,128]{4,0,3,2,1:T(8,128)S(1)} %fusion.161, f32[12,4,3,128,128]{4,3,2,1,0:T(8,128)} %param.18), kind=kOutput, calls=%fused_computation.74 | convolution fusion | flops 169869312 | bytes 9695232 | tf_op jit(solution)/shard_map/bkdij,cebkj->cedbi/dot_general | solution.py:65
  42.7 34.1 %all-reduce.1 = (f32[2]{0:T(128)S(1)}, f32[2]{0:T(128)S(1)}) all-reduce(f32[2]{0:T(128)S(1)} %multiply_reduce_fusion.21, f32[2]{0:T(128)S(1)} %multiply_reduce_fusion.20), channel_id=1, replica_groups=mesh['tile'=16,'case'=2] {'tile'}, use_global_device_ids=true, to_apply=%region_1.0 | all-reduce | flops 4 | bytes 32 | tf_op jit(solution)/shard_map/psum | solution.py:85
  76.9 29.5 %psum.184 = f32[2]{0:T(128)S(1)} all-reduce(f32[2]{0:T(128)S(1)} %get-tuple-element.69), channel_id=1, replica_groups=mesh['tile'=16,'case'=2] {'tile'}, use_global_device_ids=true, to_apply=%region_5.7 | all-reduce | flops 2 | bytes 16 | tf_op jit(solution)/shard_map/psum | solution.py:85
  112.4 10.5 fusion.46
  123.1 7.3 fusion.20
  138.4 31.5 %psum.185 = f32[2]{0:T(128)S(1)} all-reduce(f32[2]{0:T(128)S(1)} %get-tuple-element.65), channel_id=1, replica_groups=mesh['tile'=16,'case'=2] {'tile'}, use_global_device_ids=true, to_apply=%region_7.9 | all-reduce | flops 2 | bytes 16 | tf_op jit(solution)/shard_map/psum | solution.py:82
  170.1 29.5 %psum.186 = f32[2]{0:T(128)S(1)} all-reduce(f32[2]{0:T(128)S(1)} %get-tuple-element.63), channel_id=1, replica_groups=mesh['tile'=16,'case'=2] {'tile'}, use_global_device_ids=true, to_apply=%region_9.11 | all-reduce | flops 2 | bytes 16 | tf_op jit(solution)/shard_map/psum | solution.py:85
  205.5 10.5 fusion.44
  216.2 7.3 fusion.18
  231.5 31.5 %psum.187 = f32[2]{0:T(128)S(1)} all-reduce(f32[2]{0:T(128)S(1)} %get-tuple-element.59), channel_id=1, replica_groups=mesh['tile'=16,'case'=2] {'tile'}, use_global_device_ids=true, to_apply=%region_11.13 | all-reduce | flops 2 | bytes 16 | tf_op jit(solution)/shard_map/psum | solution.py:82
  263.2 29.5 %psum.188 = f32[2]{0:T(128)S(1)} all-reduce(f32[2]{0:T(128)S(1)} %get-tuple-element.57), channel_id=1, replica_groups=mesh['tile'=16,'case'=2] {'tile'}, use_global_device_ids=true, to_apply=%region_13.15 | all-reduce | flops 2 | bytes 16 | tf_op jit(solution)/shard_map/psum | solution.py:85
  298.6 10.5 fusion.42
  309.4 7.3 fusion.16
  324.7 31.5 %psum.189 = f32[2]{0:T(128)S(1)} all-reduce(f32[2]{0:T(128)S(1)} %get-tuple-element.53), channel_id=1, replica_groups=mesh['tile'=16,'case'=2] {'tile'}, use_global_device_ids=true, to_apply=%region_15.17 | all-reduce | flops 2 | bytes 16 | tf_op jit(solution)/shard_map/psum | solution.py:82
  356.3 29.5 %psum.190 = f32[2]{0:T(128)S(1)} all-reduce(f32[2]{0:T(128)S(1)} %get-tuple-element.51), channel_id=1, replica_groups=mesh['tile'=16,'case'=2] {'tile'}, use_global_device_ids=true, to_apply=%region_17.19 | all-reduce | flops 2 | bytes 16 | tf_op jit(solution)/shard_map/psum | solution.py:85
  391.8 10.5 fusion.40
  402.5 7.3 fusion.14
  417.8 31.5 %psum.191 = f32[2]{0:T(128)S(1)} all-reduce(f32[2]{0:T(128)S(1)} %get-tuple-element.47), channel_id=1, replica_groups=mesh['tile'=16,'case'=2] {'tile'}, use_global_device_ids=true, to_apply=%region_19.21 | all-reduce | flops 2 | bytes 16 | tf_op jit(solution)/shard_map/psum | solution.py:82
  449.5 29.5 %psum.192 = f32[2]{0:T(128)S(1)} all-reduce(f32[2]{0:T(128)S(1)} %multiply_reduce_fusion.11), channel_id=1, replica_groups=mesh['tile'=16,'case'=2] {'tile'}, use_global_device_ids=true, to_apply=%region_21.23 | all-reduce | flops 2 | bytes 16 | tf_op jit(solution)/shard_map/psum | solution.py:85
  484.9 10.5 fusion.38
  495.7 7.3 fusion.12
  511.0 31.5 %psum.193 = f32[2]{0:T(128)S(1)} all-reduce(f32[2]{0:T(128)S(1)} %fusion.238), channel_id=1, replica_groups=mesh['tile'=16,'case'=2] {'tile'}, use_global_device_ids=true, to_apply=%region_23.25 | all-reduce | flops 2 | bytes 16 | tf_op jit(solution)/shard_map/psum | solution.py:82
  548.8 10.5 fusion.36
  559.6 7.3 fusion.10
  573.1 31.9 %all-reduce = (f32[2]{0:T(128)S(1)}, f32[2]{0:T(128)S(1)}) all-reduce(f32[2]{0:T(128)S(1)} %get-tuple-element.9, f32[2]{0:T(128)S(1)} %get-tuple-element.8), channel_id=1, replica_groups=mesh['tile'=16,'case'=2] {'tile'}, use_global_device_ids=true, to_apply=%region_25.27 | all-reduce | flops 4 | bytes 32 | tf_op jit(solution)/shard_map/psum | solution.py:85
  605.2 29.5 %psum.196 = f32[2]{0:T(128)S(1)} all-reduce(f32[2]{0:T(128)S(1)} %get-tuple-element.40), channel_id=1, replica_groups=mesh['tile'=16,'case'=2] {'tile'}, use_global_device_ids=true, to_apply=%region_29.31 | all-reduce | flops 2 | bytes 16 | tf_op jit(solution)/shard_map/psum | solution.py:85
  640.6 10.5 fusion.34
  651.3 7.3 fusion.8
  666.6 31.5 %psum.197 = f32[2]{0:T(128)S(1)} all-reduce(f32[2]{0:T(128)S(1)} %get-tuple-element.36), channel_id=1, replica_groups=mesh['tile'=16,'case'=2] {'tile'}, use_global_device_ids=true, to_apply=%region_31.33 | all-reduce | flops 2 | bytes 16 | tf_op jit(solution)/shard_map/psum | solution.py:82
  698.3 29.5 %psum.198 = f32[2]{0:T(128)S(1)} all-reduce(f32[2]{0:T(128)S(1)} %get-tuple-element.34), channel_id=1, replica_groups=mesh['tile'=16,'case'=2] {'tile'}, use_global_device_ids=true, to_apply=%region_33.35 | all-reduce | flops 2 | bytes 16 | tf_op jit(solution)/shard_map/psum | solution.py:85
  733.7 10.5 fusion.32
  744.5 7.3 fusion.6
  759.7 31.5 %psum.199 = f32[2]{0:T(128)S(1)} all-reduce(f32[2]{0:T(128)S(1)} %get-tuple-element.30), channel_id=1, replica_groups=mesh['tile'=16,'case'=2] {'tile'}, use_global_device_ids=true, to_apply=%region_35.37 | all-reduce | flops 2 | bytes 16 | tf_op jit(solution)/shard_map/psum | solution.py:82
  791.4 29.5 %psum.200 = f32[2]{0:T(128)S(1)} all-reduce(f32[2]{0:T(128)S(1)} %get-tuple-element.28), channel_id=1, replica_groups=mesh['tile'=16,'case'=2] {'tile'}, use_global_device_ids=true, to_apply=%region_37.39 | all-reduce | flops 2 | bytes 16 | tf_op jit(solution)/shard_map/psum | solution.py:85
  826.9 10.5 fusion.30
  837.6 7.3 fusion.4
  852.9 31.5 %psum.201 = f32[2]{0:T(128)S(1)} all-reduce(f32[2]{0:T(128)S(1)} %get-tuple-element.24), channel_id=1, replica_groups=mesh['tile'=16,'case'=2] {'tile'}, use_global_device_ids=true, to_apply=%region_39.41 | all-reduce | flops 2 | bytes 16 | tf_op jit(solution)/shard_map/psum | solution.py:82
  884.6 29.5 %psum.202 = f32[2]{0:T(128)S(1)} all-reduce(f32[2]{0:T(128)S(1)} %get-tuple-element.22), channel_id=1, replica_groups=mesh['tile'=16,'case'=2] {'tile'}, use_global_device_ids=true, to_apply=%region_41.43 | all-reduce | flops 2 | bytes 16 | tf_op jit(solution)/shard_map/psum | solution.py:85
  920.0 10.5 fusion.28
  930.7 7.3 fusion.2
  946.0 31.5 %psum.203 = f32[2]{0:T(128)S(1)} all-reduce(f32[2]{0:T(128)S(1)} %get-tuple-element.18), channel_id=1, replica_groups=mesh['tile'=16,'case'=2] {'tile'}, use_global_device_ids=true, to_apply=%region_43.45 | all-reduce | flops 2 | bytes 16 | tf_op jit(solution)/shard_map/psum | solution.py:82
  977.7 29.5 %psum.204 = f32[2]{0:T(128)S(1)} all-reduce(f32[2]{0:T(128)S(1)} %multiply_reduce_fusion), channel_id=1, replica_groups=mesh['tile'=16,'case'=2] {'tile'}, use_global_device_ids=true, to_apply=%region_45.47 | all-reduce | flops 2 | bytes 16 | tf_op jit(solution)/shard_map/psum | solution.py:85
  1013.2 10.5 fusion.26
  1023.9 7.3 fusion
  1039.2 31.5 %psum.205 = f32[2]{0:T(128)S(1)} all-reduce(f32[2]{0:T(128)S(1)} %fusion.224), channel_id=1, replica_groups=mesh['tile'=16,'case'=2] {'tile'}, use_global_device_ids=true, to_apply=%region_47.49 | all-reduce | flops 2 | bytes 16 | tf_op jit(solution)/shard_map/psum | solution.py:82
  1077.0 10.5 fusion.50
  1087.8 8.7 all-reduce.2
  (353 shorter events, 185.9 us)
Async XLA Ops:
  2.1 13.4 %collective-permute-start = (f32[2,3,12,128]{3,2,1,0:T(8,128)S(1)}, f32[2,3,12,128]{3,2,1,0:T(8,128)S(1)}, u32[]{:S(2)}, u32[]{:S(2)}) collective-permute-start(f32[2,3,12,128]{3,2,1,0:T(8,128)S(1)} %broadcast_multiply_fusion.11), channel_id=1, source_target_pairs={{0,2},{2,4},{4,6},{6,8},{8,10},{10,12},{12,14},{14,16},{16,18},{18... | collective-permute-start | bytes 110600 | tf_op jit(solution)/shard_map/ppermute | solution.py:18
  4.5 11.6 %collective-permute-start.2 = (f32[2,3,12,128]{3,2,1,0:T(8,128)S(1)}, f32[2,3,12,128]{3,2,1,0:T(8,128)S(1)}, u32[]{:S(2)}, u32[]{:S(2)}) collective-permute-start(f32[2,3,12,128]{3,2,1,0:T(8,128)S(1)} %broadcast_multiply_fusion.11), channel_id=1, source_target_pairs={{2,0},{4,2},{6,4},{8,6},{10,8},{12,10},{14,12},{16,14},{18,16},{20... | collective-permute-start | bytes 110600 | tf_op jit(solution)/shard_map/ppermute | solution.py:19
  5.8 7.2 collective-permute-start.1
  11.0 4.5 collective-permute-start.3
  35.2 6.6 collective-permute-start.5
  36.8 5.7 collective-permute-start.4
  106.5 3.2 collective-permute-start.6
  108.3 3.1 collective-permute-start.7
  131.3 6.1 collective-permute-start.9
  132.6 5.7 collective-permute-start.8
  199.6 3.3 collective-permute-start.10
  201.4 3.1 collective-permute-start.11
  224.4 6.1 collective-permute-start.13
  225.7 5.7 collective-permute-start.12
  292.8 3.3 collective-permute-start.14
  294.5 3.1 collective-permute-start.15
  317.5 6.1 collective-permute-start.17
  318.8 5.7 collective-permute-start.16
  385.9 3.4 collective-permute-start.18
  387.7 3.1 collective-permute-start.19
  410.7 6.1 collective-permute-start.21
  412.0 5.7 collective-permute-start.20
  479.1 3.6 collective-permute-start.22
  480.8 3.1 collective-permute-start.23
  503.8 6.1 collective-permute-start.25
  505.1 5.7 collective-permute-start.24
  542.6 4.5 collective-permute-start.27
  543.9 3.9 collective-permute-start.26
  567.7 4.3 collective-permute-start.29
  569.0 3.9 collective-permute-start.28
  634.7 3.3 collective-permute-start.30
  636.5 3.1 collective-permute-start.31
  659.5 6.1 collective-permute-start.33
  660.8 5.7 collective-permute-start.32
  727.9 3.3 collective-permute-start.34
  752.6 6.1 collective-permute-start.37
  753.9 5.7 collective-permute-start.36
  821.0 3.4 collective-permute-start.38
  845.8 6.1 collective-permute-start.41
  847.1 5.7 collective-permute-start.40
  914.1 3.6 collective-permute-start.42
  938.9 6.1 collective-permute-start.45
  940.2 5.7 collective-permute-start.44
  1007.3 3.3 collective-permute-start.46
  1032.1 6.1 collective-permute-start.49
  1033.4 5.7 collective-permute-start.48
  1070.8 3.3 collective-permute-start.50
  1072.8 3.2 collective-permute-start.51
  (9 other events, 155.8 us)
where the time goes:
time: 1110 us; the launch traced here: 1100 us
  blocking collectives  684 us (62%)
  matrix products  238 us (21%)
  starting transfers between devices  122 us (11%)
  waiting for transfers between devices  22 us (2%)
  local copies, waits for them, and re-layouts  17.9 us (2%)
    psum x12, blocking collectives, squares(): return lax.psum(jnp.sum(residual * residual, axis=(1, 2, 3)), 'tile')  361 us
    psum x10, blocking collectives, curvature(): return lax.psum(jnp.sum(first * second, axis=(1, 2, 3)), 'tile')  315 us
    dot_general x13, matrix products, strains(): return jnp.einsum('bkdij,cebkj->cedbi', smooth, gathered, precision=HIGH)  138 us
    ppermute x26, starting transfers between devices, extended(): before = lax.ppermute(last, axis, up)  85.9 us
    dot_general x12, matrix products, operate(): contrib = jnp.einsum('bkdij,cedbi->cebkj', smooth, stress, precision=HIGH)  84.8 us
    ppermute x26, starting transfers between devices, extended(): after = lax.ppermute(leading, axis, down)  36.5 us
  transfers between devices with their start and end apart: 52, of which 24 were waited for; matrix products, arithmetic and copies ran while one was open for 1% of the time, Pallas kernels for 0%

commit v1 on v0

--- a/solution.py
+++ b/solution.py
@@ -82,7 +82,7 @@
         return lax.psum(jnp.sum(first * second, axis=(1, 2, 3)), "tile")
 
     def squares(residual):
-        return lax.psum(jnp.sum(residual * residual, axis=(1, 2, 3)), "tile")
+        return jnp.sum(lax.all_gather(jnp.sum(residual * residual, axis=(1, 2, 3)), "tile"), axis=0)
 
     def widen(scalars):
         return scalars[:, None, None, None]

time: 1110 us -> 1110 us (level)
    psum x12 -> x0, blocking collectives: 361 us -> none  [squares(): return lax.psum(jnp.sum(residual * residual, axis=(1, 2, 3)), 'tile')]
    unnamed x0 -> x12, blocking collectives: none -> 360 us
  transfers between devices with their start and end apart: 52 -> 52, of which waited for: 24 -> 23; matrix products, arithmetic and copies ran while one was open for 1% -> 1% of each run, Pallas kernels for 0% -> 0%
where the time goes in v1:
time: 1110 us; the launch traced here: 1100 us
  blocking collectives  683 us (62%)
  matrix products  238 us (21%)
  starting transfers between devices  122 us (11%)
  local copies, waits for them, and re-layouts  22 us (2%)
  waiting for transfers between devices  21.5 us (2%)
    unnamed x12, blocking collectives  360 us
    psum x10, blocking collectives, curvature(): return lax.psum(jnp.sum(first * second, axis=(1, 2, 3)), 'tile')  315 us
    dot_general x13, matrix products, strains(): return jnp.einsum('bkdij,cebkj->cedbi', smooth, gathered, precision=HIGH)  138 us
    ppermute x26, starting transfers between devices, extended(): before = lax.ppermute(last, axis, up)  86 us
    dot_general x12, matrix products, operate(): contrib = jnp.einsum('bkdij,cedbi->cebkj', smooth, stress, precision=HIGH)  84.8 us
    ppermute x26, starting transfers between devices, extended(): after = lax.ppermute(leading, axis, down)  36.3 us
  transfers between devices with their start and end apart: 52, of which 23 were waited for; matrix products, arithmetic and copies ran while one was open for 1% of the time, Pallas kernels for 0%

profile of v1, /device:TPU:0, one launch (start us, length us, event | category | flops | bytes accessed | tf_op | source)
XLA Modules:
  0.0 1100.6 jit_solution(5524224031820667939)
XLA Ops:
  5.8 5.1 collective-permute-start.1
  18.0 11.6 %fusion.48 = f32[12,2,3,3,128,1]{4,2,5,3,1,0:T(4,128)S(1)} fusion(f32[12,4,2,3,128]{4,0,3,2,1:T(8,128)S(1)} %fusion.161, f32[12,4,3,128,128]{4,3,2,1,0:T(8,128)} %param.18), kind=kOutput, calls=%fused_computation.74 | convolution fusion | flops 169869312 | bytes 9695232 | tf_op jit(solution)/shard_map/bkdij,cebkj->cedbi/dot_general | solution.py:65
  43.5 33.3 %all-reduce.13 = (f32[32]{0:T(128)S(1)}, f32[2]{0:T(128)S(1)}) all-reduce(f32[32]{0:T(128)S(1)} %dynamic-update-slice, f32[2]{0:T(128)S(1)} %multiply_reduce_fusion.20), channel_id=2, replica_groups=mesh['tile'=16,'case'=2] {'tile'}, use_global_device_ids=true, to_apply=%add | all-reduce | flops 34 | bytes 272
  77.3 29.5 %all-reduce.1 = f32[32]{0:T(128)S(1)} all-reduce(f32[32]{0:T(128)S(1)} %dynamic-update-slice.1), channel_id=3, replica_groups=mesh['tile'=16,'case'=2] {'tile'}, use_global_device_ids=true, to_apply=%add.1 | all-reduce | flops 32 | bytes 256
  112.8 10.5 fusion.46
  123.5 7.3 fusion.20
  138.8 31.5 %psum.99 = f32[2]{0:T(128)S(1)} all-reduce(f32[2]{0:T(128)S(1)} %get-tuple-element.65), channel_id=1, replica_groups=mesh['tile'=16,'case'=2] {'tile'}, use_global_device_ids=true, to_apply=%region_7.9 | all-reduce | flops 2 | bytes 16 | tf_op jit(solution)/shard_map/psum | solution.py:82
  170.7 29.5 %all-reduce.2 = f32[32]{0:T(128)S(1)} all-reduce(f32[32]{0:T(128)S(1)} %dynamic-update-slice.2), channel_id=4, replica_groups=mesh['tile'=16,'case'=2] {'tile'}, use_global_device_ids=true, to_apply=%add.2 | all-reduce | flops 32 | bytes 256
  206.3 10.5 fusion.44
  217.0 7.3 fusion.18
  232.3 31.5 %psum.100 = f32[2]{0:T(128)S(1)} all-reduce(f32[2]{0:T(128)S(1)} %get-tuple-element.59), channel_id=1, replica_groups=mesh['tile'=16,'case'=2] {'tile'}, use_global_device_ids=true, to_apply=%region_11.13 | all-reduce | flops 2 | bytes 16 | tf_op jit(solution)/shard_map/psum | solution.py:82
  264.2 29.5 %all-reduce.3 = f32[32]{0:T(128)S(1)} all-reduce(f32[32]{0:T(128)S(1)} %dynamic-update-slice.3), channel_id=5, replica_groups=mesh['tile'=16,'case'=2] {'tile'}, use_global_device_ids=true, to_apply=%add.3 | all-reduce | flops 32 | bytes 256
  299.7 10.5 fusion.42
  310.5 7.3 fusion.16
  325.8 31.5 %psum.101 = f32[2]{0:T(128)S(1)} all-reduce(f32[2]{0:T(128)S(1)} %get-tuple-element.53), channel_id=1, replica_groups=mesh['tile'=16,'case'=2] {'tile'}, use_global_device_ids=true, to_apply=%region_15.17 | all-reduce | flops 2 | bytes 16 | tf_op jit(solution)/shard_map/psum | solution.py:82
  357.6 29.5 %all-reduce.4 = f32[32]{0:T(128)S(1)} all-reduce(f32[32]{0:T(128)S(1)} %dynamic-update-slice.4), channel_id=6, replica_groups=mesh['tile'=16,'case'=2] {'tile'}, use_global_device_ids=true, to_apply=%add.4 | all-reduce | flops 32 | bytes 256
  393.2 10.5 fusion.40
  403.9 7.3 fusion.14
  419.2 31.5 %psum.102 = f32[2]{0:T(128)S(1)} all-reduce(f32[2]{0:T(128)S(1)} %get-tuple-element.47), channel_id=1, replica_groups=mesh['tile'=16,'case'=2] {'tile'}, use_global_device_ids=true, to_apply=%region_19.21 | all-reduce | flops 2 | bytes 16 | tf_op jit(solution)/shard_map/psum | solution.py:82
  451.1 29.5 %all-reduce.5 = f32[32]{0:T(128)S(1)} all-reduce(f32[32]{0:T(128)S(1)} %dynamic-update-slice.5), channel_id=7, replica_groups=mesh['tile'=16,'case'=2] {'tile'}, use_global_device_ids=true, to_apply=%add.5 | all-reduce | flops 32 | bytes 256
  486.7 10.5 fusion.38
  497.4 7.3 fusion.12
  512.7 31.5 %psum.103 = f32[2]{0:T(128)S(1)} all-reduce(f32[2]{0:T(128)S(1)} %fusion.238), channel_id=1, replica_groups=mesh['tile'=16,'case'=2] {'tile'}, use_global_device_ids=true, to_apply=%region_23.25 | all-reduce | flops 2 | bytes 16 | tf_op jit(solution)/shard_map/psum | solution.py:82
  550.6 10.5 fusion.36
  561.4 7.3 fusion.10
  575.1 31.8 %all-reduce.12 = (f32[32]{0:T(128)S(1)}, f32[2]{0:T(128)S(1)}) all-reduce(f32[32]{0:T(128)S(1)} %dynamic-update-slice.6, f32[2]{0:T(128)S(1)} %get-tuple-element.8), channel_id=8, replica_groups=mesh['tile'=16,'case'=2] {'tile'}, use_global_device_ids=true, to_apply=%add.6 | all-reduce | flops 34 | bytes 272
  607.4 29.5 %all-reduce.7 = f32[32]{0:T(128)S(1)} all-reduce(f32[32]{0:T(128)S(1)} %dynamic-update-slice.7), channel_id=9, replica_groups=mesh['tile'=16,'case'=2] {'tile'}, use_global_device_ids=true, to_apply=%add.7 | all-reduce | flops 32 | bytes 256
  643.0 10.5 fusion.34
  653.7 7.3 fusion.8
  669.0 31.5 %psum.105 = f32[2]{0:T(128)S(1)} all-reduce(f32[2]{0:T(128)S(1)} %get-tuple-element.36), channel_id=1, replica_groups=mesh['tile'=16,'case'=2] {'tile'}, use_global_device_ids=true, to_apply=%region_31.33 | all-reduce | flops 2 | bytes 16 | tf_op jit(solution)/shard_map/psum | solution.py:82
  700.9 29.5 %all-reduce.8 = f32[32]{0:T(128)S(1)} all-reduce(f32[32]{0:T(128)S(1)} %dynamic-update-slice.8), channel_id=10, replica_groups=mesh['tile'=16,'case'=2] {'tile'}, use_global_device_ids=true, to_apply=%add.8 | all-reduce | flops 32 | bytes 256
  736.4 10.5 fusion.32
  747.2 7.3 fusion.6
  762.5 31.5 %psum.106 = f32[2]{0:T(128)S(1)} all-reduce(f32[2]{0:T(128)S(1)} %get-tuple-element.30), channel_id=1, replica_groups=mesh['tile'=16,'case'=2] {'tile'}, use_global_device_ids=true, to_apply=%region_35.37 | all-reduce | flops 2 | bytes 16 | tf_op jit(solution)/shard_map/psum | solution.py:82
  794.3 29.5 %all-reduce.9 = f32[32]{0:T(128)S(1)} all-reduce(f32[32]{0:T(128)S(1)} %dynamic-update-slice.9), channel_id=11, replica_groups=mesh['tile'=16,'case'=2] {'tile'}, use_global_device_ids=true, to_apply=%add.9 | all-reduce | flops 32 | bytes 256
  829.9 10.5 fusion.30
  840.6 7.3 fusion.4
  855.9 31.5 %psum.107 = f32[2]{0:T(128)S(1)} all-reduce(f32[2]{0:T(128)S(1)} %get-tuple-element.24), channel_id=1, replica_groups=mesh['tile'=16,'case'=2] {'tile'}, use_global_device_ids=true, to_apply=%region_39.41 | all-reduce | flops 2 | bytes 16 | tf_op jit(solution)/shard_map/psum | solution.py:82
  887.8 29.5 %all-reduce.10 = f32[32]{0:T(128)S(1)} all-reduce(f32[32]{0:T(128)S(1)} %dynamic-update-slice.10), channel_id=12, replica_groups=mesh['tile'=16,'case'=2] {'tile'}, use_global_device_ids=true, to_apply=%add.10 | all-reduce | flops 32 | bytes 256
  923.4 10.5 fusion.28
  934.1 7.3 fusion.2
  949.4 31.5 %psum.108 = f32[2]{0:T(128)S(1)} all-reduce(f32[2]{0:T(128)S(1)} %get-tuple-element.18), channel_id=1, replica_groups=mesh['tile'=16,'case'=2] {'tile'}, use_global_device_ids=true, to_apply=%region_43.45 | all-reduce | flops 2 | bytes 16 | tf_op jit(solution)/shard_map/psum | solution.py:82
  981.3 29.5 %all-reduce.11 = f32[32]{0:T(128)S(1)} all-reduce(f32[32]{0:T(128)S(1)} %dynamic-update-slice.11), channel_id=13, replica_groups=mesh['tile'=16,'case'=2] {'tile'}, use_global_device_ids=true, to_apply=%add.11 | all-reduce | flops 32 | bytes 256
  1016.8 10.5 fusion.26
  1027.6 7.3 fusion
  1042.9 31.5 %psum.109 = f32[2]{0:T(128)S(1)} all-reduce(f32[2]{0:T(128)S(1)} %fusion.224), channel_id=1, replica_groups=mesh['tile'=16,'case'=2] {'tile'}, use_global_device_ids=true, to_apply=%region_47.49 | all-reduce | flops 2 | bytes 16 | tf_op jit(solution)/shard_map/psum | solution.py:82
  1080.7 10.5 fusion.50
  1091.4 8.7 all-reduce.14
  (404 shorter events, 189.7 us)
Async XLA Ops:
  2.1 13.4 %collective-permute-start = (f32[2,3,12,128]{3,2,1,0:T(8,128)S(1)}, f32[2,3,12,128]{3,2,1,0:T(8,128)S(1)}, u32[]{:S(2)}, u32[]{:S(2)}) collective-permute-start(f32[2,3,12,128]{3,2,1,0:T(8,128)S(1)} %broadcast_multiply_fusion.11), channel_id=1, source_target_pairs={{0,2},{2,4},{4,6},{6,8},{8,10},{10,12},{12,14},{14,16},{16,18},{18... | collective-permute-start | bytes 110600 | tf_op jit(solution)/shard_map/ppermute | solution.py:18
  4.5 11.6 %collective-permute-start.2 = (f32[2,3,12,128]{3,2,1,0:T(8,128)S(1)}, f32[2,3,12,128]{3,2,1,0:T(8,128)S(1)}, u32[]{:S(2)}, u32[]{:S(2)}) collective-permute-start(f32[2,3,12,128]{3,2,1,0:T(8,128)S(1)} %broadcast_multiply_fusion.11), channel_id=1, source_target_pairs={{2,0},{4,2},{6,4},{8,6},{10,8},{12,10},{14,12},{16,14},{18,16},{20... | collective-permute-start | bytes 110600 | tf_op jit(solution)/shard_map/ppermute | solution.py:19
  5.8 7.2 collective-permute-start.1
  11.0 4.5 collective-permute-start.3
  35.2 8.1 collective-permute-start.5
  36.8 6.5 collective-permute-start.4
  106.9 3.3 collective-permute-start.6
  108.7 3.1 collective-permute-start.7
  131.7 6.1 collective-permute-start.9
  133.0 5.7 collective-permute-start.8
  200.4 3.3 collective-permute-start.10
  225.2 6.1 collective-permute-start.13
  226.5 5.7 collective-permute-start.12
  293.9 3.5 collective-permute-start.14
  295.6 3.1 collective-permute-start.15
  318.6 6.1 collective-permute-start.17
  319.9 5.7 collective-permute-start.16
  387.3 3.3 collective-permute-start.18
  389.1 3.1 collective-permute-start.19
  412.1 6.1 collective-permute-start.21
  413.4 5.7 collective-permute-start.20
  480.8 3.3 collective-permute-start.22
  482.6 3.1 collective-permute-start.23
  505.6 6.1 collective-permute-start.25
  506.9 5.7 collective-permute-start.24
  544.4 4.6 collective-permute-start.27
  545.7 4.0 collective-permute-start.26
  569.5 4.3 collective-permute-start.29
  570.8 3.9 collective-permute-start.28
  637.1 3.5 collective-permute-start.30
  638.9 3.1 collective-permute-start.31
  661.9 6.1 collective-permute-start.33
  663.2 5.7 collective-permute-start.32
  730.6 3.3 collective-permute-start.34
  732.3 3.1 collective-permute-start.35
  755.3 6.1 collective-permute-start.37
  756.6 5.7 collective-permute-start.36
  824.0 3.3 collective-permute-start.38
  848.8 6.1 collective-permute-start.41
  850.1 5.7 collective-permute-start.40
  917.5 3.3 collective-permute-start.42
  942.3 6.1 collective-permute-start.45
  943.6 5.7 collective-permute-start.44
  1010.9 3.4 collective-permute-start.46
  1035.7 6.1 collective-permute-start.49
  1037.0 5.7 collective-permute-start.48
  1074.5 3.3 collective-permute-start.50
  1076.4 3.2 collective-permute-start.51
  (10 other events, 179.7 us)
